TPU v7x, 256 devices: a whole 4x4x8 slice. The times are simulated.
256 devices in a mesh: segment: 4 (over y), blk: 64 (over x, z, core).
Axes of the slice: x: 4, y: 4, z: 8, core: 2. Of those that a mesh axis runs over, the one named last changes fastest.
Arguments:
- inputs: bfloat16 [4, 1024, 64, 128], P(None, 'blk'), may hold values from -6 to 6
- weights: bfloat16 [8, 1024, 64, 2048], P('segment', 'blk'), may hold values from -0.1875 to 0.1875
- biases: float32 [8, 1024, 64], P('segment', 'blk'), may hold values from -3 to 3
- tile_index: int32 [8, 1024, 32], P('segment', 'blk'), may hold values from 0 to 31, each once within a row
Outputs:
- final_activity: bfloat16 [4, 1024, 64, 128], P('segment', 'blk')
Inputs may be any that keep to these rules, and one draw needn't show every extreme that they name: `tile_index`: each row of 32 entries names every member 0..31 once.
All inputs are finite; a program needn't handle non-finite values.
Results may differ from a plain program's by a relative error of at most 0.014.
Values may be sent and summed in bfloat16 or wider, within the bound.
A program may use at most 128 MiB of HBM per device.

v0:
```python
import jax
import jax.numpy as jnp
from jax import lax
from jax.sharding import PartitionSpec as P


def from_partner(array, axis, stride):
    return lax.ppermute(array, axis, [(i, i ^ 1 << stride) for i in range(lax.axis_size(axis))])


def passed_along(value, axis, steps):
    count = lax.axis_size(axis)
    initial, last = (max(0, -steps), min(count, count - steps))
    return lax.ppermute(value, axis, [(source, source + steps) for source in range(initial, last)])


def permuted_weights(weights, tile_index):
    blocks, tile_size, row_width = weights.shape
    fan_count = tile_index.shape[1]
    shaped = weights.reshape(blocks, tile_size, fan_count, row_width // fan_count)
    onehot = (
        tile_index[:, :, None] == jnp.arange(fan_count, dtype=jnp.int32)[None, None, :]
    ).astype(jnp.bfloat16)
    placed = jnp.einsum("jakc,jkm->jamc", shaped, onehot, preferred_element_type=jnp.float32)
    return placed.astype(jnp.bfloat16).reshape(blocks * tile_size, row_width)


def join_group(activity, bit_place):
    partner = from_partner(activity, "blk", bit_place)
    upper_half = lax.axis_index("blk") // (1 << bit_place) % 2
    first_order = jnp.concatenate([activity, partner], axis=0)
    second = jnp.concatenate([partner, activity], axis=0)
    return jnp.where(upper_half == 0, first_order, second)


def apply_layer(activity, bit_place, matrix, offset):
    grouped = join_group(activity, bit_place)
    members, tile_size, batch_size = grouped.shape
    flat_group = grouped.reshape(members * tile_size, batch_size)
    summed = jnp.dot(matrix, flat_group, preferred_element_type=jnp.float32)
    summed = summed.reshape(activity.shape) + offset[:, :, None]
    return jnp.maximum(summed, 0.0).astype(jnp.bfloat16)


def regroup_segmented(activity, group_size):
    local_blocks, tile_size, batch_size = activity.shape
    position = lax.axis_index("blk")
    for level_index in range(group_size.bit_length() - 1):
        shaped = activity.reshape(
            local_blocks >> level_index + 1, 2, 1 << level_index, tile_size, batch_size
        )
        own_bit = (position >> level_index + 1) % 2
        outgoing = lax.dynamic_index_in_dim(shaped, 1 - own_bit, 1, keepdims=True)
        incoming = from_partner(outgoing, "blk", level_index + 1)
        shaped = lax.dynamic_update_index_in_dim(shaped, incoming, 1 - own_bit, 1)
        activity = shaped.reshape(local_blocks, tile_size, batch_size)
    return activity


def body(inputs, weights, biases, tile_index):
    segments = lax.axis_size("segment")
    segment_index = lax.axis_index("segment")
    devices = lax.axis_size("blk")
    local_blocks = inputs.shape[1]
    group_size = min(local_blocks, devices // 4)
    far_bit = (2 * group_size).bit_length() - 1
    micro_count = inputs.shape[0]
    matrices = [
        permuted_weights(weights[layer_index], tile_index[layer_index]) for layer_index in range(2)
    ]
    results = jnp.zeros(inputs.shape, jnp.bfloat16)
    arriving = jnp.zeros(inputs.shape[1:], jnp.bfloat16)
    step_count = micro_count + segments - 1
    for step_index in range(step_count):
        new_input = inputs[min(step_index, micro_count - 1)]
        present = jnp.where(segment_index == 0, new_input, arriving)
        present = apply_layer(present, 0, matrices[0], biases[0])
        present = regroup_segmented(present, group_size)
        present = apply_layer(present, far_bit, matrices[1], biases[1])
        present = regroup_segmented(present, group_size)
        finished = step_index - (segments - 1)
        if finished >= 0:
            results = results.at[finished].set(present)
        if step_index + 1 < step_count:
            arriving = passed_along(present, "segment", 1)
    gathered = lax.all_to_all(results[:, None], "segment", split_axis=0, concat_axis=1, tiled=True)
    return gathered[:, segments - 1]


def solution(mesh):
    in_specs = (
        P(None, "blk", None, None),
        P("segment", "blk", None, None),
        P("segment", "blk", None),
        P("segment", "blk", None),
    )
    out_specs = P("segment", "blk", None, None)
    return jax.shard_map(body, mesh=mesh, in_specs=in_specs, out_specs=out_specs, check_vma=False)
```

profile of v0, /device:TPU:26, one launch (start us, length us, event | category | flops | bytes accessed | tf_op | source)
XLA Modules:
  0.0 688.3 jit_solution(18264248735898804815)
XLA Ops:
  7.4 12.9 %reshape_squeeze.7 = bf16[16,64,32,64]{3,2,1,0:T(8,128)(2,1)} reshape(bf16[1,16,64,2048]{3,2,1,0:T(8,128)(2,1)} %get-tuple-element.53) | data formatting | bytes 8388608 | tf_op jit(solution)/shard_map/reshape;squeeze | solution.py:20
  20.3 9.1 %convert_bitcast_fusion = bf16[16,64,32,64]{3,2,1,0:T(8,128)(2,1)} fusion(bf16[16,64,32,64]{3,2,1,0:T(8,128)(2,1)} %reshape_squeeze.7, s32[16,32]{1,0:T(8,128)S(1)} %get-tuple-element.57), kind=kOutput, calls=%fused_computation | convolution fusion | flops 136331264 | bytes 8390656 | tf_op jit(solution)/shard_map/jakc,jkm->jamc/dot_general | solution.py:24
  29.4 9.2 %fusion.163 = bf16[16,64,128]{2,1,0:T(8,128)(2,1)S(1)} fusion(bf16[16,64,32,64]{3,2,1,0:T(8,128)(2,1)} %convert_bitcast_fusion, bf16[16,64,128]{2,1,0:T(8,128)(2,1)S(1)} %collective-permute-done, bf16[16,64,128]{2,1,0:T(8,128)(2,1)S(1)} %select_bitcast_fusion, pred[]{:T(512)S(6)} %eq.137, f32[16,64]{1,0:T(8,128)S(1)} %get-tuple-element.56), kind=kOutput, calls=%fused_computation.75 | convolution fusion | flops 538050560 | bytes 4984833 | tf_op jit(solution)/shard_map/dot_general | solution.py:40
  54.4 6.8 collective-permute-start.3
  68.0 12.9 %reshape_squeeze.6 = bf16[16,64,32,64]{3,2,1,0:T(8,128)(2,1)} reshape(bf16[1,16,64,2048]{3,2,1,0:T(8,128)(2,1)} %get-tuple-element.54) | data formatting | bytes 8388608 | tf_op jit(solution)/shard_map/reshape;squeeze | solution.py:20
  83.2 9.1 %convert_bitcast_fusion.1 = bf16[16,64,32,64]{3,2,1,0:T(8,128)(2,1)} fusion(bf16[16,64,32,64]{3,2,1,0:T(8,128)(2,1)} %reshape_squeeze.6, s32[16,32]{1,0:T(8,128)S(1)} %get-tuple-element.58), kind=kOutput, calls=%fused_computation.1 | convolution fusion | flops 136331264 | bytes 8390656 | tf_op jit(solution)/shard_map/jakc,jkm->jamc/dot_general | solution.py:24
  92.3 9.2 %fusion.184 = bf16[16,64,128]{2,1,0:T(8,128)(2,1)S(1)} fusion(bf16[16,64,32,64]{3,2,1,0:T(8,128)(2,1)} %convert_bitcast_fusion.1, bf16[16,64,128]{2,1,0:T(8,128)(2,1)S(1)} %collective-permute-done.5, bf16[16,64,128]{2,1,0:T(8,128)(2,1)S(1)} %bitcast.344, pred[]{:T(512)S(6)} %eq.132, f32[16,64]{1,0:T(8,128)S(1)} %get-tuple-element.55), kind=kOutput, calls=%fused_computation.82 | convolution fusion | flops 538050560 | bytes 4984833 | tf_op jit(solution)/shard_map/dot_general | solution.py:40
  117.2 7.4 %collective-permute-done.8 = bf16[2,1,4,64,128]{4,3,2,1,0:T(8,128)(2,1)S(1)} collective-permute-done((bf16[2,1,4,64,128]{4,3,2,1,0:T(8,128)(2,1)S(1)}, bf16[2,1,4,64,128]{4,3,2,1,0:T(8,128)(2,1)S(1)}, u32[]{:S(2)}, u32[]{:S(2)}) %collective-permute-start.8) | collective-permute-done | bytes 131104 | tf_op jit(solution)/shard_map/ppermute | solution.py:8
  131.0 7.0 %collective-permute-done.10 = bf16[16,64,128]{2,1,0:T(8,128)(2,1)S(1)} collective-permute-done((bf16[16,64,128]{2,1,0:T(8,128)(2,1)S(1)}, bf16[16,64,128]{2,1,0:T(8,128)(2,1)S(1)}, u32[]{:S(2)}, u32[]{:S(2)}) %collective-permute-start.10) | collective-permute-done | bytes 262176 | tf_op jit(solution)/shard_map/ppermute | solution.py:14
  139.6 10.0 %fusion.160 = bf16[16,64,128]{2,1,0:T(8,128)(2,1)S(1)} fusion(bf16[16,64,32,64]{3,2,1,0:T(8,128)(2,1)} %convert_bitcast_fusion, bf16[16,64,128]{2,1,0:T(8,128)(2,1)S(1)} %collective-permute-done.11, bf16[16,64,128]{2,1,0:T(8,128)(2,1)S(1)} %bitcast_select_fusion, pred[]{:T(512)S(6)} %eq.137, f32[16,64]{1,0:T(8,128)S(1)} %get-tuple-element.56), kind=kOutput, calls=%fused_computation.74 | convolution fusion | flops 538050560 | bytes 4984833 | tf_op jit(solution)/shard_map/dot_general | solution.py:40
  165.2 7.4 %collective-permute-done.14 = bf16[2,1,4,64,128]{4,3,2,1,0:T(8,128)(2,1)S(1)} collective-permute-done((bf16[2,1,4,64,128]{4,3,2,1,0:T(8,128)(2,1)S(1)}, bf16[2,1,4,64,128]{4,3,2,1,0:T(8,128)(2,1)S(1)}, u32[]{:S(2)}, u32[]{:S(2)}) %collective-permute-start.14) | collective-permute-done | bytes 131104 | tf_op jit(solution)/shard_map/ppermute | solution.py:8
  221.4 7.0 %collective-permute-done.21 = bf16[16,64,128]{2,1,0:T(8,128)(2,1)S(1)} collective-permute-done((bf16[16,64,128]{2,1,0:T(8,128)(2,1)S(1)}, bf16[16,64,128]{2,1,0:T(8,128)(2,1)S(1)}, u32[]{:S(2)}, u32[]{:S(2)}) %collective-permute-start.21) | collective-permute-done | bytes 262176 | tf_op jit(solution)/shard_map/ppermute | solution.py:14
  254.3 7.9 %collective-permute-done.25 = bf16[2,1,4,64,128]{4,3,2,1,0:T(8,128)(2,1)S(1)} collective-permute-done((bf16[2,1,4,64,128]{4,3,2,1,0:T(8,128)(2,1)S(1)}, bf16[2,1,4,64,128]{4,3,2,1,0:T(8,128)(2,1)S(1)}, u32[]{:S(2)}, u32[]{:S(2)}) %collective-permute-start.25) | collective-permute-done | bytes 131104 | tf_op jit(solution)/shard_map/ppermute | solution.py:8
  269.1 7.7 %collective-permute-done.27 = bf16[16,64,128]{2,1,0:T(8,128)(2,1)S(1)} collective-permute-done((bf16[16,64,128]{2,1,0:T(8,128)(2,1)S(1)}, bf16[16,64,128]{2,1,0:T(8,128)(2,1)S(1)}, u32[]{:S(2)}, u32[]{:S(2)}) %collective-permute-start.27) | collective-permute-done | bytes 262176 | tf_op jit(solution)/shard_map/ppermute | solution.py:8
  297.4 6.9 %collective-permute-done.30 = bf16[2,1,4,64,128]{4,3,2,1,0:T(8,128)(2,1)S(1)} collective-permute-done((bf16[2,1,4,64,128]{4,3,2,1,0:T(8,128)(2,1)S(1)}, bf16[2,1,4,64,128]{4,3,2,1,0:T(8,128)(2,1)S(1)}, u32[]{:S(2)}, u32[]{:S(2)}) %collective-permute-start.30) | collective-permute-done | bytes 131104 | tf_op jit(solution)/shard_map/ppermute | solution.py:8
  310.8 7.0 %collective-permute-done.32 = bf16[16,64,128]{2,1,0:T(8,128)(2,1)S(1)} collective-permute-done((bf16[16,64,128]{2,1,0:T(8,128)(2,1)S(1)}, bf16[16,64,128]{2,1,0:T(8,128)(2,1)S(1)}, u32[]{:S(2)}, u32[]{:S(2)}) %collective-permute-start.32) | collective-permute-done | bytes 262176 | tf_op jit(solution)/shard_map/ppermute | solution.py:14
  345.1 7.9 %collective-permute-done.36 = bf16[2,1,4,64,128]{4,3,2,1,0:T(8,128)(2,1)S(1)} collective-permute-done((bf16[2,1,4,64,128]{4,3,2,1,0:T(8,128)(2,1)S(1)}, bf16[2,1,4,64,128]{4,3,2,1,0:T(8,128)(2,1)S(1)}, u32[]{:S(2)}, u32[]{:S(2)}) %collective-permute-start.36) | collective-permute-done | bytes 131104 | tf_op jit(solution)/shard_map/ppermute | solution.py:8
  359.4 7.1 %collective-permute-done.38 = bf16[16,64,128]{2,1,0:T(8,128)(2,1)S(1)} collective-permute-done((bf16[16,64,128]{2,1,0:T(8,128)(2,1)S(1)}, bf16[16,64,128]{2,1,0:T(8,128)(2,1)S(1)}, u32[]{:S(2)}, u32[]{:S(2)}) %collective-permute-start.38) | collective-permute-done | bytes 262176 | tf_op jit(solution)/shard_map/ppermute | solution.py:8
  388.3 7.1 %collective-permute-done.41 = bf16[2,1,4,64,128]{4,3,2,1,0:T(8,128)(2,1)S(1)} collective-permute-done((bf16[2,1,4,64,128]{4,3,2,1,0:T(8,128)(2,1)S(1)}, bf16[2,1,4,64,128]{4,3,2,1,0:T(8,128)(2,1)S(1)}, u32[]{:S(2)}, u32[]{:S(2)}) %collective-permute-start.41) | collective-permute-done | bytes 131104 | tf_op jit(solution)/shard_map/ppermute | solution.py:8
  401.9 7.0 %collective-permute-done.43 = bf16[16,64,128]{2,1,0:T(8,128)(2,1)S(1)} collective-permute-done((bf16[16,64,128]{2,1,0:T(8,128)(2,1)S(1)}, bf16[16,64,128]{2,1,0:T(8,128)(2,1)S(1)}, u32[]{:S(2)}, u32[]{:S(2)}) %collective-permute-start.43) | collective-permute-done | bytes 262176 | tf_op jit(solution)/shard_map/ppermute | solution.py:14
  436.0 7.9 %collective-permute-done.47 = bf16[2,1,4,64,128]{4,3,2,1,0:T(8,128)(2,1)S(1)} collective-permute-done((bf16[2,1,4,64,128]{4,3,2,1,0:T(8,128)(2,1)S(1)}, bf16[2,1,4,64,128]{4,3,2,1,0:T(8,128)(2,1)S(1)}, u32[]{:S(2)}, u32[]{:S(2)}) %collective-permute-start.47) | collective-permute-done | bytes 131104 | tf_op jit(solution)/shard_map/ppermute | solution.py:8
  450.0 7.2 %collective-permute-done.49 = bf16[16,64,128]{2,1,0:T(8,128)(2,1)S(1)} collective-permute-done((bf16[16,64,128]{2,1,0:T(8,128)(2,1)S(1)}, bf16[16,64,128]{2,1,0:T(8,128)(2,1)S(1)}, u32[]{:S(2)}, u32[]{:S(2)}) %collective-permute-start.49) | collective-permute-done | bytes 262176 | tf_op jit(solution)/shard_map/ppermute | solution.py:8
  479.0 7.2 %collective-permute-done.52 = bf16[2,1,4,64,128]{4,3,2,1,0:T(8,128)(2,1)S(1)} collective-permute-done((bf16[2,1,4,64,128]{4,3,2,1,0:T(8,128)(2,1)S(1)}, bf16[2,1,4,64,128]{4,3,2,1,0:T(8,128)(2,1)S(1)}, u32[]{:S(2)}, u32[]{:S(2)}) %collective-permute-start.52) | collective-permute-done | bytes 131104 | tf_op jit(solution)/shard_map/ppermute | solution.py:8
  492.6 7.0 %collective-permute-done.54 = bf16[16,64,128]{2,1,0:T(8,128)(2,1)S(1)} collective-permute-done((bf16[16,64,128]{2,1,0:T(8,128)(2,1)S(1)}, bf16[16,64,128]{2,1,0:T(8,128)(2,1)S(1)}, u32[]{:S(2)}, u32[]{:S(2)}) %collective-permute-start.54) | collective-permute-done | bytes 262176 | tf_op jit(solution)/shard_map/ppermute | solution.py:14
  526.9 7.9 %collective-permute-done.58 = bf16[2,1,4,64,128]{4,3,2,1,0:T(8,128)(2,1)S(1)} collective-permute-done((bf16[2,1,4,64,128]{4,3,2,1,0:T(8,128)(2,1)S(1)}, bf16[2,1,4,64,128]{4,3,2,1,0:T(8,128)(2,1)S(1)}, u32[]{:S(2)}, u32[]{:S(2)}) %collective-permute-start.58) | collective-permute-done | bytes 131104 | tf_op jit(solution)/shard_map/ppermute | solution.py:8
  540.9 7.1 %collective-permute-done.60 = bf16[16,64,128]{2,1,0:T(8,128)(2,1)S(1)} collective-permute-done((bf16[16,64,128]{2,1,0:T(8,128)(2,1)S(1)}, bf16[16,64,128]{2,1,0:T(8,128)(2,1)S(1)}, u32[]{:S(2)}, u32[]{:S(2)}) %collective-permute-start.60) | collective-permute-done | bytes 262176 | tf_op jit(solution)/shard_map/ppermute | solution.py:8
  569.9 7.2 %collective-permute-done.63 = bf16[2,1,4,64,128]{4,3,2,1,0:T(8,128)(2,1)S(1)} collective-permute-done((bf16[2,1,4,64,128]{4,3,2,1,0:T(8,128)(2,1)S(1)}, bf16[2,1,4,64,128]{4,3,2,1,0:T(8,128)(2,1)S(1)}, u32[]{:S(2)}, u32[]{:S(2)}) %collective-permute-start.63) | collective-permute-done | bytes 131104 | tf_op jit(solution)/shard_map/ppermute | solution.py:8
  583.4 7.0 %collective-permute-done.65 = bf16[16,64,128]{2,1,0:T(8,128)(2,1)S(1)} collective-permute-done((bf16[16,64,128]{2,1,0:T(8,128)(2,1)S(1)}, bf16[16,64,128]{2,1,0:T(8,128)(2,1)S(1)}, u32[]{:S(2)}, u32[]{:S(2)}) %collective-permute-start.65) | collective-permute-done | bytes 262176 | tf_op jit(solution)/shard_map/ppermute | solution.py:14
  617.6 7.9 %collective-permute-done.69 = bf16[2,1,4,64,128]{4,3,2,1,0:T(8,128)(2,1)S(1)} collective-permute-done((bf16[2,1,4,64,128]{4,3,2,1,0:T(8,128)(2,1)S(1)}, bf16[2,1,4,64,128]{4,3,2,1,0:T(8,128)(2,1)S(1)}, u32[]{:S(2)}, u32[]{:S(2)}) %collective-permute-start.69) | collective-permute-done | bytes 131104 | tf_op jit(solution)/shard_map/ppermute | solution.py:8
  631.6 7.2 %collective-permute-done.71 = bf16[16,64,128]{2,1,0:T(8,128)(2,1)S(1)} collective-permute-done((bf16[16,64,128]{2,1,0:T(8,128)(2,1)S(1)}, bf16[16,64,128]{2,1,0:T(8,128)(2,1)S(1)}, u32[]{:S(2)}, u32[]{:S(2)}) %collective-permute-start.71) | collective-permute-done | bytes 262176 | tf_op jit(solution)/shard_map/ppermute | solution.py:8
  660.8 7.0 %collective-permute-done.74 = bf16[2,1,4,64,128]{4,3,2,1,0:T(8,128)(2,1)S(1)} collective-permute-done((bf16[2,1,4,64,128]{4,3,2,1,0:T(8,128)(2,1)S(1)}, bf16[2,1,4,64,128]{4,3,2,1,0:T(8,128)(2,1)S(1)}, u32[]{:S(2)}, u32[]{:S(2)}) %collective-permute-start.74) | collective-permute-done | bytes 131104 | tf_op jit(solution)/shard_map/ppermute | solution.py:8
  673.0 14.2 %all_to_all.12 = bf16[4,1,16,64,128]{4,3,2,1,0:T(8,128)(2,1)S(1)} all-to-all(bf16[4,1,16,64,128]{4,3,2,1,0:T(8,128)(2,1)S(1)} %bitcast_dynamic-update-slice_fusion), channel_id=1, replica_groups=mesh['segment'=4,'blk'=64] {'segment'}, dimensions={0} | all-to-all | bytes 2097152 | tf_op jit(solution)/shard_map/all_to_all | solution.py:86
  (282 shorter events, 426.3 us)
Async XLA Ops:
  1.0 28.4 %collective-permute-start = (bf16[16,64,128]{2,1,0:T(8,128)(2,1)S(1)}, bf16[16,64,128]{2,1,0:T(8,128)(2,1)S(1)}, u32[]{:S(2)}, u32[]{:S(2)}) collective-permute-start(bf16[16,64,128]{2,1,0:T(8,128)(2,1)S(1)} %select_bitcast_fusion), channel_id=1, source_target_pairs={{0,1},{1,0},{2,3},{3,2},{4,5},{5,4},{6,7},{7,6},{8,9},{9,8},{10,11... | collective-permute-start | bytes 786440 | tf_op jit(solution)/shard_map/ppermute | solution.py:8
  44.8 9.6 %collective-permute-start.2 = (bf16[4,1,2,64,128]{4,3,2,1,0:T(8,128)(2,1)S(1)}, bf16[4,1,2,64,128]{4,3,2,1,0:T(8,128)(2,1)S(1)}, u32[]{:S(2)}, u32[]{:S(2)}) collective-permute-start(bf16[4,1,2,64,128]{4,3,2,1,0:T(8,128)(2,1)S(1)} %constant_dynamic-slice_fusion.54), channel_id=1, source_target_pairs={{0,4},{1,5},{2,6},{3,7},{4,0},{5,1},{6,2},{7,3},{8,12},{9,13},{10,... | collective-permute-start | bytes 393224 | tf_op jit(solution)/shard_map/ppermute | solution.py:8
  54.4 12.8 %collective-permute-start.3 = (bf16[2,1,4,64,128]{4,3,2,1,0:T(8,128)(2,1)S(1)}, bf16[2,1,4,64,128]{4,3,2,1,0:T(8,128)(2,1)S(1)}, u32[]{:S(2)}, u32[]{:S(2)}) collective-permute-start(bf16[2,1,4,64,128]{4,3,2,1,0:T(8,128)(2,1)S(1)} %constant_dynamic-slice_fusion.53), channel_id=1, source_target_pairs={{0,8},{1,9},{2,10},{3,11},{4,12},{5,13},{6,14},{7,15},{8,0},{9,1},... | collective-permute-start | bytes 393224 | tf_op jit(solution)/shard_map/ppermute | solution.py:8
  67.3 13.5 %collective-permute-start.4 = (bf16[1,1,8,64,128]{4,3,2,1,0:T(8,128)(2,1)S(1)}, bf16[1,1,8,64,128]{4,3,2,1,0:T(8,128)(2,1)S(1)}, u32[]{:S(2)}, u32[]{:S(2)}) collective-permute-start(bf16[1,1,8,64,128]{4,3,2,1,0:T(8,128)(2,1)S(1)} %constant_dynamic-slice_fusion.52), channel_id=1, source_target_pairs={{0,16},{1,17},{2,18},{3,19},{4,20},{5,21},{6,22},{7,23},{8,24},{9,... | collective-permute-start | bytes 393224 | tf_op jit(solution)/shard_map/ppermute | solution.py:8
  80.8 11.4 %collective-permute-start.5 = (bf16[16,64,128]{2,1,0:T(8,128)(2,1)S(1)}, bf16[16,64,128]{2,1,0:T(8,128)(2,1)S(1)}, u32[]{:S(2)}, u32[]{:S(2)}) collective-permute-start(bf16[16,64,128]{2,1,0:T(8,128)(2,1)S(1)} %bitcast.343), channel_id=1, source_target_pairs={{0,32},{1,33},{2,34},{3,35},{4,36},{5,37},{6,38},{7,39},{8,40},{9,... | collective-permute-start | bytes 786440 | tf_op jit(solution)/shard_map/ppermute | solution.py:8
  114.2 10.4 %collective-permute-start.8 = (bf16[2,1,4,64,128]{4,3,2,1,0:T(8,128)(2,1)S(1)}, bf16[2,1,4,64,128]{4,3,2,1,0:T(8,128)(2,1)S(1)}, u32[]{:S(2)}, u32[]{:S(2)}) collective-permute-start(bf16[2,1,4,64,128]{4,3,2,1,0:T(8,128)(2,1)S(1)} %constant_dynamic-slice_fusion.49), channel_id=1, source_target_pairs={{0,8},{1,9},{2,10},{3,11},{4,12},{5,13},{6,14},{7,15},{8,0},{9,1},... | collective-permute-start | bytes 393224 | tf_op jit(solution)/shard_map/ppermute | solution.py:8
  129.7 8.3 %collective-permute-start.10 = (bf16[16,64,128]{2,1,0:T(8,128)(2,1)S(1)}, bf16[16,64,128]{2,1,0:T(8,128)(2,1)S(1)}, u32[]{:S(2)}, u32[]{:S(2)}) collective-permute-start(bf16[16,64,128]{2,1,0:T(8,128)(2,1)S(1)} %bitcast.363), channel_id=1, source_target_pairs={{0,64},{64,128},{128,192},{1,65},{65,129},{129,193},{2,66},{66,130... | collective-permute-start | bytes 786440 | tf_op jit(solution)/shard_map/ppermute | solution.py:14
  162.2 10.4 %collective-permute-start.14 = (bf16[2,1,4,64,128]{4,3,2,1,0:T(8,128)(2,1)S(1)}, bf16[2,1,4,64,128]{4,3,2,1,0:T(8,128)(2,1)S(1)}, u32[]{:S(2)}, u32[]{:S(2)}) collective-permute-start(bf16[2,1,4,64,128]{4,3,2,1,0:T(8,128)(2,1)S(1)} %constant_dynamic-slice_fusion.45), channel_id=1, source_target_pairs={{0,8},{1,9},{2,10},{3,11},{4,12},{5,13},{6,14},{7,15},{8,0},{9,1},... | collective-permute-start | bytes 393224 | tf_op jit(solution)/shard_map/ppermute | solution.py:8
  203.2 9.1 %collective-permute-start.19 = (bf16[2,1,4,64,128]{4,3,2,1,0:T(8,128)(2,1)S(1)}, bf16[2,1,4,64,128]{4,3,2,1,0:T(8,128)(2,1)S(1)}, u32[]{:S(2)}, u32[]{:S(2)}) collective-permute-start(bf16[2,1,4,64,128]{4,3,2,1,0:T(8,128)(2,1)S(1)} %constant_dynamic-slice_fusion.41), channel_id=1, source_target_pairs={{0,8},{1,9},{2,10},{3,11},{4,12},{5,13},{6,14},{7,15},{8,0},{9,1},... | collective-permute-start | bytes 393224 | tf_op jit(solution)/shard_map/ppermute | solution.py:8
  220.1 8.3 %collective-permute-start.21 = (bf16[16,64,128]{2,1,0:T(8,128)(2,1)S(1)}, bf16[16,64,128]{2,1,0:T(8,128)(2,1)S(1)}, u32[]{:S(2)}, u32[]{:S(2)}) collective-permute-start(bf16[16,64,128]{2,1,0:T(8,128)(2,1)S(1)} %bitcast.382), channel_id=1, source_target_pairs={{0,64},{64,128},{128,192},{1,65},{65,129},{129,193},{2,66},{66,130... | collective-permute-start | bytes 786440 | tf_op jit(solution)/shard_map/ppermute | solution.py:14
  242.3 8.5 %collective-permute-start.24 = (bf16[4,1,2,64,128]{4,3,2,1,0:T(8,128)(2,1)S(1)}, bf16[4,1,2,64,128]{4,3,2,1,0:T(8,128)(2,1)S(1)}, u32[]{:S(2)}, u32[]{:S(2)}) collective-permute-start(bf16[4,1,2,64,128]{4,3,2,1,0:T(8,128)(2,1)S(1)} %constant_dynamic-slice_fusion.38), channel_id=1, source_target_pairs={{0,4},{1,5},{2,6},{3,7},{4,0},{5,1},{6,2},{7,3},{8,12},{9,13},{10,... | collective-permute-start | bytes 393224 | tf_op jit(solution)/shard_map/ppermute | solution.py:8
  250.9 11.3 %collective-permute-start.25 = (bf16[2,1,4,64,128]{4,3,2,1,0:T(8,128)(2,1)S(1)}, bf16[2,1,4,64,128]{4,3,2,1,0:T(8,128)(2,1)S(1)}, u32[]{:S(2)}, u32[]{:S(2)}) collective-permute-start(bf16[2,1,4,64,128]{4,3,2,1,0:T(8,128)(2,1)S(1)} %constant_dynamic-slice_fusion.37), channel_id=1, source_target_pairs={{0,8},{1,9},{2,10},{3,11},{4,12},{5,13},{6,14},{7,15},{8,0},{9,1},... | collective-permute-start | bytes 393224 | tf_op jit(solution)/shard_map/ppermute | solution.py:8
  267.7 9.1 %collective-permute-start.27 = (bf16[16,64,128]{2,1,0:T(8,128)(2,1)S(1)}, bf16[16,64,128]{2,1,0:T(8,128)(2,1)S(1)}, u32[]{:S(2)}, u32[]{:S(2)}) collective-permute-start(bf16[16,64,128]{2,1,0:T(8,128)(2,1)S(1)} %bitcast.391), channel_id=1, source_target_pairs={{0,32},{1,33},{2,34},{3,35},{4,36},{5,37},{6,38},{7,39},{8,40},{9,... | collective-permute-start | bytes 786440 | tf_op jit(solution)/shard_map/ppermute | solution.py:8
  294.4 10.0 %collective-permute-start.30 = (bf16[2,1,4,64,128]{4,3,2,1,0:T(8,128)(2,1)S(1)}, bf16[2,1,4,64,128]{4,3,2,1,0:T(8,128)(2,1)S(1)}, u32[]{:S(2)}, u32[]{:S(2)}) collective-permute-start(bf16[2,1,4,64,128]{4,3,2,1,0:T(8,128)(2,1)S(1)} %constant_dynamic-slice_fusion.33), channel_id=1, source_target_pairs={{0,8},{1,9},{2,10},{3,11},{4,12},{5,13},{6,14},{7,15},{8,0},{9,1},... | collective-permute-start | bytes 393224 | tf_op jit(solution)/shard_map/ppermute | solution.py:8
  309.5 8.3 %collective-permute-start.32 = (bf16[16,64,128]{2,1,0:T(8,128)(2,1)S(1)}, bf16[16,64,128]{2,1,0:T(8,128)(2,1)S(1)}, u32[]{:S(2)}, u32[]{:S(2)}) collective-permute-start(bf16[16,64,128]{2,1,0:T(8,128)(2,1)S(1)} %bitcast.401), channel_id=1, source_target_pairs={{0,64},{64,128},{128,192},{1,65},{65,129},{129,193},{2,66},{66,130... | collective-permute-start | bytes 786440 | tf_op jit(solution)/shard_map/ppermute | solution.py:14
  332.3 9.7 %collective-permute-start.35 = (bf16[4,1,2,64,128]{4,3,2,1,0:T(8,128)(2,1)S(1)}, bf16[4,1,2,64,128]{4,3,2,1,0:T(8,128)(2,1)S(1)}, u32[]{:S(2)}, u32[]{:S(2)}) collective-permute-start(bf16[4,1,2,64,128]{4,3,2,1,0:T(8,128)(2,1)S(1)} %constant_dynamic-slice_fusion.30), channel_id=1, source_target_pairs={{0,4},{1,5},{2,6},{3,7},{4,0},{5,1},{6,2},{7,3},{8,12},{9,13},{10,... | collective-permute-start | bytes 393224 | tf_op jit(solution)/shard_map/ppermute | solution.py:8
  342.1 10.9 %collective-permute-start.36 = (bf16[2,1,4,64,128]{4,3,2,1,0:T(8,128)(2,1)S(1)}, bf16[2,1,4,64,128]{4,3,2,1,0:T(8,128)(2,1)S(1)}, u32[]{:S(2)}, u32[]{:S(2)}) collective-permute-start(bf16[2,1,4,64,128]{4,3,2,1,0:T(8,128)(2,1)S(1)} %constant_dynamic-slice_fusion.29), channel_id=1, source_target_pairs={{0,8},{1,9},{2,10},{3,11},{4,12},{5,13},{6,14},{7,15},{8,0},{9,1},... | collective-permute-start | bytes 393224 | tf_op jit(solution)/shard_map/ppermute | solution.py:8
  358.1 8.4 %collective-permute-start.38 = (bf16[16,64,128]{2,1,0:T(8,128)(2,1)S(1)}, bf16[16,64,128]{2,1,0:T(8,128)(2,1)S(1)}, u32[]{:S(2)}, u32[]{:S(2)}) collective-permute-start(bf16[16,64,128]{2,1,0:T(8,128)(2,1)S(1)} %bitcast.410), channel_id=1, source_target_pairs={{0,32},{1,33},{2,34},{3,35},{4,36},{5,37},{6,38},{7,39},{8,40},{9,... | collective-permute-start | bytes 786440 | tf_op jit(solution)/shard_map/ppermute | solution.py:8
  385.3 10.2 %collective-permute-start.41 = (bf16[2,1,4,64,128]{4,3,2,1,0:T(8,128)(2,1)S(1)}, bf16[2,1,4,64,128]{4,3,2,1,0:T(8,128)(2,1)S(1)}, u32[]{:S(2)}, u32[]{:S(2)}) collective-permute-start(bf16[2,1,4,64,128]{4,3,2,1,0:T(8,128)(2,1)S(1)} %constant_dynamic-slice_fusion.25), channel_id=1, source_target_pairs={{0,8},{1,9},{2,10},{3,11},{4,12},{5,13},{6,14},{7,15},{8,0},{9,1},... | collective-permute-start | bytes 393224 | tf_op jit(solution)/shard_map/ppermute | solution.py:8
  400.6 8.3 %collective-permute-start.43 = (bf16[16,64,128]{2,1,0:T(8,128)(2,1)S(1)}, bf16[16,64,128]{2,1,0:T(8,128)(2,1)S(1)}, u32[]{:S(2)}, u32[]{:S(2)}) collective-permute-start(bf16[16,64,128]{2,1,0:T(8,128)(2,1)S(1)} %bitcast.303), channel_id=1, source_target_pairs={{0,64},{64,128},{128,192},{1,65},{65,129},{129,193},{2,66},{66,130... | collective-permute-start | bytes 786440 | tf_op jit(solution)/shard_map/ppermute | solution.py:14
  422.9 10.0 %collective-permute-start.46 = (bf16[4,1,2,64,128]{4,3,2,1,0:T(8,128)(2,1)S(1)}, bf16[4,1,2,64,128]{4,3,2,1,0:T(8,128)(2,1)S(1)}, u32[]{:S(2)}, u32[]{:S(2)}) collective-permute-start(bf16[4,1,2,64,128]{4,3,2,1,0:T(8,128)(2,1)S(1)} %constant_dynamic-slice_fusion.22), channel_id=1, source_target_pairs={{0,4},{1,5},{2,6},{3,7},{4,0},{5,1},{6,2},{7,3},{8,12},{9,13},{10,... | collective-permute-start | bytes 393224 | tf_op jit(solution)/shard_map/ppermute | solution.py:8
  432.9 10.9 %collective-permute-start.47 = (bf16[2,1,4,64,128]{4,3,2,1,0:T(8,128)(2,1)S(1)}, bf16[2,1,4,64,128]{4,3,2,1,0:T(8,128)(2,1)S(1)}, u32[]{:S(2)}, u32[]{:S(2)}) collective-permute-start(bf16[2,1,4,64,128]{4,3,2,1,0:T(8,128)(2,1)S(1)} %constant_dynamic-slice_fusion.21), channel_id=1, source_target_pairs={{0,8},{1,9},{2,10},{3,11},{4,12},{5,13},{6,14},{7,15},{8,0},{9,1},... | collective-permute-start | bytes 393224 | tf_op jit(solution)/shard_map/ppermute | solution.py:8
  475.9 10.2 %collective-permute-start.52 = (bf16[2,1,4,64,128]{4,3,2,1,0:T(8,128)(2,1)S(1)}, bf16[2,1,4,64,128]{4,3,2,1,0:T(8,128)(2,1)S(1)}, u32[]{:S(2)}, u32[]{:S(2)}) collective-permute-start(bf16[2,1,4,64,128]{4,3,2,1,0:T(8,128)(2,1)S(1)} %constant_dynamic-slice_fusion.17), channel_id=1, source_target_pairs={{0,8},{1,9},{2,10},{3,11},{4,12},{5,13},{6,14},{7,15},{8,0},{9,1},... | collective-permute-start | bytes 393224 | tf_op jit(solution)/shard_map/ppermute | solution.py:8
  491.3 8.3 %collective-permute-start.54 = (bf16[16,64,128]{2,1,0:T(8,128)(2,1)S(1)}, bf16[16,64,128]{2,1,0:T(8,128)(2,1)S(1)}, u32[]{:S(2)}, u32[]{:S(2)}) collective-permute-start(bf16[16,64,128]{2,1,0:T(8,128)(2,1)S(1)} %bitcast.322), channel_id=1, source_target_pairs={{0,64},{64,128},{128,192},{1,65},{65,129},{129,193},{2,66},{66,130... | collective-permute-start | bytes 786440 | tf_op jit(solution)/shard_map/ppermute | solution.py:14
  513.8 10.0 %collective-permute-start.57 = (bf16[4,1,2,64,128]{4,3,2,1,0:T(8,128)(2,1)S(1)}, bf16[4,1,2,64,128]{4,3,2,1,0:T(8,128)(2,1)S(1)}, u32[]{:S(2)}, u32[]{:S(2)}) collective-permute-start(bf16[4,1,2,64,128]{4,3,2,1,0:T(8,128)(2,1)S(1)} %constant_dynamic-slice_fusion.14), channel_id=1, source_target_pairs={{0,4},{1,5},{2,6},{3,7},{4,0},{5,1},{6,2},{7,3},{8,12},{9,13},{10,... | collective-permute-start | bytes 393224 | tf_op jit(solution)/shard_map/ppermute | solution.py:8
  523.9 10.9 %collective-permute-start.58 = (bf16[2,1,4,64,128]{4,3,2,1,0:T(8,128)(2,1)S(1)}, bf16[2,1,4,64,128]{4,3,2,1,0:T(8,128)(2,1)S(1)}, u32[]{:S(2)}, u32[]{:S(2)}) collective-permute-start(bf16[2,1,4,64,128]{4,3,2,1,0:T(8,128)(2,1)S(1)} %constant_dynamic-slice_fusion.13), channel_id=1, source_target_pairs={{0,8},{1,9},{2,10},{3,11},{4,12},{5,13},{6,14},{7,15},{8,0},{9,1},... | collective-permute-start | bytes 393224 | tf_op jit(solution)/shard_map/ppermute | solution.py:8
  566.8 10.2 %collective-permute-start.63 = (bf16[2,1,4,64,128]{4,3,2,1,0:T(8,128)(2,1)S(1)}, bf16[2,1,4,64,128]{4,3,2,1,0:T(8,128)(2,1)S(1)}, u32[]{:S(2)}, u32[]{:S(2)}) collective-permute-start(bf16[2,1,4,64,128]{4,3,2,1,0:T(8,128)(2,1)S(1)} %constant_dynamic-slice_fusion.9), channel_id=1, source_target_pairs={{0,8},{1,9},{2,10},{3,11},{4,12},{5,13},{6,14},{7,15},{8,0},{9,1},... | collective-permute-start | bytes 393224 | tf_op jit(solution)/shard_map/ppermute | solution.py:8
  582.1 8.3 %collective-permute-start.65 = (bf16[16,64,128]{2,1,0:T(8,128)(2,1)S(1)}, bf16[16,64,128]{2,1,0:T(8,128)(2,1)S(1)}, u32[]{:S(2)}, u32[]{:S(2)}) collective-permute-start(bf16[16,64,128]{2,1,0:T(8,128)(2,1)S(1)} %bitcast.332), channel_id=1, source_target_pairs={{0,64},{64,128},{128,192},{1,65},{65,129},{129,193},{2,66},{66,130... | collective-permute-start | bytes 786440 | tf_op jit(solution)/shard_map/ppermute | solution.py:14
  604.5 10.0 %collective-permute-start.68 = (bf16[4,1,2,64,128]{4,3,2,1,0:T(8,128)(2,1)S(1)}, bf16[4,1,2,64,128]{4,3,2,1,0:T(8,128)(2,1)S(1)}, u32[]{:S(2)}, u32[]{:S(2)}) collective-permute-start(bf16[4,1,2,64,128]{4,3,2,1,0:T(8,128)(2,1)S(1)} %constant_dynamic-slice_fusion.6), channel_id=1, source_target_pairs={{0,4},{1,5},{2,6},{3,7},{4,0},{5,1},{6,2},{7,3},{8,12},{9,13},{10,... | collective-permute-start | bytes 393224 | tf_op jit(solution)/shard_map/ppermute | solution.py:8
  614.5 10.9 %collective-permute-start.69 = (bf16[2,1,4,64,128]{4,3,2,1,0:T(8,128)(2,1)S(1)}, bf16[2,1,4,64,128]{4,3,2,1,0:T(8,128)(2,1)S(1)}, u32[]{:S(2)}, u32[]{:S(2)}) collective-permute-start(bf16[2,1,4,64,128]{4,3,2,1,0:T(8,128)(2,1)S(1)} %constant_dynamic-slice_fusion.5), channel_id=1, source_target_pairs={{0,8},{1,9},{2,10},{3,11},{4,12},{5,13},{6,14},{7,15},{8,0},{9,1},... | collective-permute-start | bytes 393224 | tf_op jit(solution)/shard_map/ppermute | solution.py:8
  630.6 8.2 %collective-permute-start.71 = (bf16[16,64,128]{2,1,0:T(8,128)(2,1)S(1)}, bf16[16,64,128]{2,1,0:T(8,128)(2,1)S(1)}, u32[]{:S(2)}, u32[]{:S(2)}) collective-permute-start(bf16[16,64,128]{2,1,0:T(8,128)(2,1)S(1)} %bitcast.353), channel_id=1, source_target_pairs={{0,32},{1,33},{2,34},{3,35},{4,36},{5,37},{6,38},{7,39},{8,40},{9,... | collective-permute-start | bytes 786440 | tf_op jit(solution)/shard_map/ppermute | solution.py:8
  657.6 10.2 %collective-permute-start.74 = (bf16[2,1,4,64,128]{4,3,2,1,0:T(8,128)(2,1)S(1)}, bf16[2,1,4,64,128]{4,3,2,1,0:T(8,128)(2,1)S(1)}, u32[]{:S(2)}, u32[]{:S(2)}) collective-permute-start(bf16[2,1,4,64,128]{4,3,2,1,0:T(8,128)(2,1)S(1)} %constant_dynamic-slice_fusion.1), channel_id=1, source_target_pairs={{0,8},{1,9},{2,10},{3,11},{4,12},{5,13},{6,14},{7,15},{8,0},{9,1},... | collective-permute-start | bytes 393224 | tf_op jit(solution)/shard_map/ppermute | solution.py:8
  (51 other events, 500.6 us)
where the time goes:
time: 700 us; the launch traced here: 688 us
  waiting for transfers between devices  366 us (52%)
  starting transfers between devices  156 us (22%)
  matrix products  114 us (16%)
  local copies, waits for them, and re-layouts  35 us (5%)
  blocking collectives  14.2 us (2%)
    ppermute x70, waiting for transfers between devices, from_partner(): lax.ppermute(array, axis, [(i, i ^ 1 << stride) for i in range(lax.axis_s...  325 us
    ppermute x70, starting transfers between devices, from_partner(): lax.ppermute(array, axis, [(i, i ^ 1 << stride) for i in range(lax.axis_s...  148 us
    dot_general x14, matrix products, apply_layer(): summed = jnp.dot(matrix, flat_group, preferred_element_type=jnp.float32)  96 us
    ppermute x6, waiting for transfers between devices, passed_along(): lax.ppermute(value, axis, [(source, source + steps) for source in range(i...  41.8 us
    another operation x2, local copies, waits for them, and re-layouts, permuted_weights(): weights.reshape(blocks, tile_size, fan_count, row_width // fan_count)  25.7 us
    dot_general x2, matrix products, permuted_weights(): jnp.einsum('jakc,jkm->jamc', shaped, onehot, preferred_element_type=jnp.f...  18.1 us
    all_to_all x1, blocking collectives, body(): lax.all_to_all(results[:, None], 'segment', split_axis=0, concat_axis=1,...  14.2 us
  transfers between devices with their start and end apart: 76, of which 73 were waited for; matrix products, arithmetic and copies ran while one was open for 7% of the time, Pallas kernels for 0%

commit v1 on v0

v1 whole, which is shorter than its diff:
```python
import functools

import jax
import jax.numpy as jnp
from jax import lax
from jax.experimental import pallas as pl
from jax.experimental.pallas import tpu as pltpu
from jax.sharding import PartitionSpec as P

MESH = pl.DeviceIdType.MESH
TILE = 64
HALF = 32
FANIN = 32
LANES = 128
SLOTS = 16
ZS = 8
XS = 4
SEGS = 4
MB = 4
CHUNKS = 2 * MB
LAYERS = 2
COLUMNS = FANIN // 2


def device(segment, x, z, core):
    return {"segment": segment, "blk": (x * ZS + z) * 2 + core}


def low_lanes(shape, width, period):
    lane = lax.broadcasted_iota(jnp.int32, shape, len(shape) - 1)
    return lax.rem(lane, period) < width


def repack(upper, lower):
    low = low_lanes(upper.shape, 64, 128)
    first = jnp.where(low, upper, pltpu.roll(lower, 64, upper.ndim - 1))
    second = jnp.where(low, pltpu.roll(upper, 64, upper.ndim - 1), lower)
    return first, second


def kernel(
    source, weights, bias, inputs, out,
    raw_even, raw_odd, near, far, entering, hidden, landed, odd_in, leaving, final, staged,
    raw_sem, in_sem, entry_recv, entry_send, core_recv, core_send, z_recv, z_send, z_own,
    x_recv, x_send, x_own, final_recv, final_own,
):
    raw = (raw_even, raw_odd)
    segment = lax.axis_index("segment")
    position = lax.axis_index("blk")
    x, z, core = position // (2 * ZS), position // 2 % ZS, position % 2
    upper, inner = x // 2, x % 2
    pair = device(segment, x, z, 1 - core)
    last = segment == SEGS - 1
    first = segment == 0

    def remote(src, dst, send, recv, target):
        return pltpu.make_async_remote_copy(
            src_ref=src, dst_ref=dst, send_sem=send, recv_sem=recv,
            device_id=target, device_id_type=MESH,
        )

    barrier = pltpu.get_barrier_semaphore()

    def greet(target):
        pl.semaphore_signal(barrier, inc=1, device_id=target, device_id_type=MESH)

    greet(pair)
    for step in (2, 1, 3):
        greet(device(segment, (x + step) % XS, z, core))
    for step in (4, 3, 5, 2, 6, 1, 7):
        greet(device(segment, x, (z + step) % ZS, core))

    @pl.when(segment > 0)
    def _():
        for step in (4, 3, 5, 2, 6, 1, 7, 0):
            for other in range(2):
                greet(device(segment - 1, 2 * upper + other, (z + step) % ZS, core))

    def raw_start(layer):
        for column in range(COLUMNS):
            pltpu.make_async_copy(
                weights.at[layer, :, :, pl.ds(column * LANES, LANES)],
                raw[layer].at[0, :, column], raw_sem.at[layer],
            ).start()

    def raw_copy(layer):
        return pltpu.make_async_copy(raw[layer].at[1], raw[layer].at[0], raw_sem.at[layer])

    def in_copy(batch):
        return pltpu.make_async_copy(inputs.at[batch], staged.at[batch], in_sem.at[batch])

    raw_start(0)

    @pl.when(first)
    def _():
        for batch in range(MB):
            in_copy(batch).start()

    raw_start(1)

    def arrange(layer):
        tiles = raw[layer]
        raw_copy(layer).wait()

        def turn(slot, carry):
            for column in range(COLUMNS):
                tiles[1, slot, column] = pltpu.roll(tiles[0, slot, column], 64, 1)
            return carry

        lax.fori_loop(0, SLOTS, turn, 0)

        def one_slot(slot, carry):
            row = (layer * SLOTS + slot) * FANIN
            rows = pl.ds(pl.multiple_of(slot * TILE, TILE), TILE)
            low = low_lanes((TILE, LANES), 64, 128)
            quarter = low_lanes((TILE, LANES), 32, 64)

            def tile_at(member, half):
                tile = source[row + member]
                return tiles[(tile + half) % 2, slot, tile // 2]

            for quad in range(FANIN // 4):
                even = jnp.where(low, tile_at(4 * quad, 0), tile_at(4 * quad + 2, 1))
                odd = jnp.where(low, tile_at(4 * quad + 1, 0), tile_at(4 * quad + 3, 1))
                lanes = pl.ds(quad * LANES, LANES)
                near[layer, rows, lanes] = jnp.where(quarter, even, pltpu.roll(odd, 32, 1))
                far[layer, rows, lanes] = jnp.where(quarter, pltpu.roll(even, 96, 1), odd)
            return carry

        lax.fori_loop(0, SLOTS, one_slot, 0)

    arrange(0)

    @pl.when(first)
    def _():
        for batch in range(MB):
            in_copy(batch).wait()

        def pack(step, carry):
            batch, block = step // SLOTS, step % SLOTS
            one, two = repack(
                staged[batch, block, pl.ds(0, HALF), :], staged[batch, block, pl.ds(HALF, HALF), :]
            )
            entering[2 * batch, core, block] = one
            entering[2 * batch + 1, core, block] = two
            return carry

        lax.fori_loop(0, MB * SLOTS, pack, 0)

    pl.semaphore_wait(barrier, 11 + jnp.where(last, 0, 16))

    low = low_lanes((HALF, LANES), 64, 128)

    def multiply(layer, values, block, store):
        rows = pl.ds(pl.multiple_of(block * 4 * TILE, 4 * TILE), 4 * TILE)
        one = jnp.dot(near[layer, rows, :], values, preferred_element_type=jnp.float32)
        two = jnp.dot(far[layer, rows, :], values, preferred_element_type=jnp.float32)
        for slot in range(4):
            a, b, c = slot * TILE, slot * TILE + HALF, (slot + 1) * TILE
            kept = jnp.where(low, one[a:b], two[b:c])
            moved = jnp.where(low, one[b:c], two[a:b])
            total = kept + pltpu.roll(moved, 64, 1) + bias[layer, block * 4 + slot]
            store(slot, jnp.maximum(total, 0.0).astype(jnp.bfloat16))

    def core_copy(chunk):
        return remote(
            entering.at[chunk, core], entering.at[chunk, core],
            core_send.at[chunk], core_recv.at[chunk], pair,
        )

    def entry_done(chunk):
        return remote(
            leaving.at[chunk], entering.at[chunk, core],
            entry_send.at[chunk], entry_recv.at[chunk], pair,
        )

    def z_done(chunk):
        span = pl.ds(0, ZS - 1)
        return remote(
            hidden.at[chunk, :, span], landed.at[chunk, :, span],
            z_send.at[chunk], z_recv.at[chunk], pair,
        )

    def z_local(chunk):
        return pltpu.make_async_copy(
            hidden.at[chunk, :, z], landed.at[chunk, :, z], z_own.at[chunk]
        )

    def x_local(chunk):
        return pltpu.make_async_copy(
            landed.at[chunk, inner], odd_in.at[chunk, x], x_own.at[chunk]
        )

    def x_done(chunk):
        span = pl.ds(0, XS - 1)
        return remote(
            odd_in.at[chunk, span], odd_in.at[chunk, span],
            x_send.at[chunk], x_recv.at[chunk], pair,
        )

    def even_layer(chunk):
        @pl.when(segment > 0)
        def _():
            entry_done(chunk).wait_recv()

        core_copy(chunk).start()
        core_copy(chunk).wait_recv()
        values = entering[chunk].reshape(FANIN * HALF, LANES)
        for turn in range(2):
            part = (z // 4 + 1 + turn) % 2
            for other in range(2):
                def store(slot, block):
                    hidden[chunk, other, part * 4 + slot] = block

                multiply(0, values, 2 * other + part, store)
            for step in range(4):
                to = part * 4 + step

                @pl.when(to != z)
                def _():
                    remote(
                        hidden.at[chunk, :, to], landed.at[chunk, :, z],
                        z_send.at[chunk], z_recv.at[chunk], device(segment, x, to, core),
                    ).start()

                @pl.when(to == z)
                def _():
                    z_local(chunk).start()

    def spread(chunk):
        z_local(chunk).wait()
        z_done(chunk).wait_recv()
        for step in (2, 1, 3):
            to = (x + step) % XS
            remote(
                landed.at[chunk, to % 2], odd_in.at[chunk, x],
                x_send.at[chunk], x_recv.at[chunk], device(segment, to, z, core),
            ).start()
        x_local(chunk).start()

    def odd_layer(chunk):
        x_local(chunk).wait()
        x_done(chunk).wait_recv()
        values = odd_in[chunk].reshape(FANIN * HALF, LANES)
        goal = chunk // 2
        for turn in range(2):
            part = (z // 4 + 1 + turn) % 2
            for other in range(2):
                def store(slot, block):
                    leaving[chunk, other, part * 4 + slot] = block

                multiply(1, values, 2 * other + part, store)
                for step in range(4):
                    to = part * 4 + step
                    block = leaving.at[chunk, other, to]

                    @pl.when(segment < SEGS - 1)
                    def _():
                        remote(
                            block, entering.at[chunk, core, inner * ZS + z],
                            entry_send.at[chunk], entry_recv.at[chunk],
                            device(segment + 1, 2 * upper + other, to, core),
                        ).start()

                    @pl.when(last)
                    def _():
                        stays = (goal == SEGS - 1) & (to == z) & (other == inner)

                        @pl.when(jnp.logical_not(stays))
                        def _():
                            remote(
                                block, final.at[chunk % 2, inner * ZS + z],
                                entry_send.at[chunk], final_recv.at[chunk % 2],
                                device(goal, 2 * upper + other, to, core),
                            ).start()

                        @pl.when(stays)
                        def _():
                            pltpu.make_async_copy(
                                block, final.at[chunk % 2, inner * ZS + z],
                                final_own.at[chunk % 2],
                            ).start()

    def step(index, carry):
        @pl.when(index < CHUNKS)
        def _():
            even_layer(index)

        @pl.when(index == 0)
        def _():
            arrange(1)

        @pl.when(index > 0)
        def _():
            odd_layer(index - 1)

        @pl.when(index < CHUNKS)
        def _():
            spread(index)

        return carry

    lax.fori_loop(0, CHUNKS + 1, step, 0)

    def final_done(half, count):
        span = pl.ds(0, count)
        return remote(
            final.at[half, span], final.at[half, span],
            entry_send.at[half], final_recv.at[half], pair,
        )

    @pl.when(segment < SEGS - 1)
    def _():
        for half in range(2):
            final_done(half, SLOTS).wait_recv()

    @pl.when(last)
    def _():
        for half in range(2):
            final_done(half, SLOTS - 1).wait_recv()
            pltpu.make_async_copy(final.at[half, 0], final.at[half, 0], final_own.at[half]).wait()

    def unpack(block, carry):
        one, two = repack(final[0, block], final[1, block])
        out[block, pl.ds(0, HALF), :] = one
        out[block, pl.ds(HALF, HALF), :] = two
        return carry

    lax.fori_loop(0, SLOTS, unpack, 0)

    def drain(chunk, carry):
        core_copy(chunk).wait_send()
        z_done(chunk).wait_send()
        x_done(chunk).wait_send()
        whole = jnp.logical_not(last & (chunk // 2 == SEGS - 1))

        @pl.when(whole)
        def _():
            entry_done(chunk).wait_send()

        @pl.when(jnp.logical_not(whole))
        def _():
            span = pl.ds(0, SLOTS - 1)
            remote(
                final.at[0, span], final.at[0, span],
                entry_send.at[chunk], final_recv.at[0], pair,
            ).wait_send()

        return carry

    lax.fori_loop(0, CHUNKS, drain, 0)


def body(inputs, weights, biases, tile_index):
    order = jnp.arange(FANIN, dtype=jnp.int32)
    source = jnp.sum(
        jnp.where(tile_index[..., :, None] == order, order[:, None], 0), axis=-2, dtype=jnp.int32
    )
    parts = biases.reshape(LAYERS, SLOTS, 2, HALF).transpose(0, 1, 3, 2)
    bias = jnp.broadcast_to(parts[..., None], (LAYERS, SLOTS, HALF, 2, LANES // 2))
    bias = bias.reshape(LAYERS, SLOTS, HALF, LANES)
    dma = pltpu.SemaphoreType.DMA
    packed = (HALF, LANES)
    vmem = lambda *shape: pltpu.VMEM(shape, jnp.bfloat16)
    result = pl.pallas_call(
        kernel,
        out_shape=jax.ShapeDtypeStruct((SLOTS, TILE, LANES), jnp.bfloat16),
        in_specs=[
            pl.BlockSpec(memory_space=pltpu.SMEM),
            pl.BlockSpec(memory_space=pl.ANY),
            pl.BlockSpec(memory_space=pltpu.VMEM),
            pl.BlockSpec(memory_space=pl.ANY),
        ],
        out_specs=pl.BlockSpec(memory_space=pltpu.VMEM),
        scratch_shapes=[
            vmem(2, SLOTS, COLUMNS, TILE, LANES),
            vmem(2, SLOTS, COLUMNS, TILE, LANES),
            vmem(LAYERS, SLOTS * TILE, FANIN * HALF),
            vmem(LAYERS, SLOTS * TILE, FANIN * HALF),
            vmem(CHUNKS, 2, SLOTS, *packed),
            vmem(CHUNKS, 2, ZS, *packed),
            vmem(CHUNKS, 2, ZS, *packed),
            vmem(CHUNKS, XS, ZS, *packed),
            vmem(CHUNKS, 2, ZS, *packed),
            vmem(2, SLOTS, *packed),
            vmem(MB, SLOTS, TILE, LANES),
            dma((LAYERS,)),
            dma((MB,)),
        ]
        + [dma((CHUNKS,))] * 10
        + [dma((2,)), dma((2,))],
        compiler_params=pltpu.CompilerParams(
            has_side_effects=True, collective_id=0, vmem_limit_bytes=60 * 1024 * 1024
        ),
    )(source.reshape(-1), weights, bias, inputs)
    return result[None]


def solution(mesh):
    in_specs = (
        P(None, "blk", None, None),
        P("segment", "blk", None, None),
        P("segment", "blk", None),
        P("segment", "blk", None),
    )
    out_specs = P("segment", "blk", None, None)
    return jax.shard_map(body, mesh=mesh, in_specs=in_specs, out_specs=out_specs, check_vma=False)
```

time: 700 us -> 175 us (0.25); the launches traced: 688 us -> 175 us
  waiting for transfers between devices: 366 us -> 0 us
  Pallas kernels: 0 us -> 168 us
  starting transfers between devices: 156 us -> 0 us
  matrix products: 114 us -> 0 us
  local copies, waits for them, and re-layouts: 35 us -> 6.03 us
  blocking collectives: 14.2 us -> 0 us
    ppermute x76 -> x0, waiting for transfers between devices: 366 us -> none  [the longest x70 325 us: from_partner(): lax.ppermute(array, axis, [(i, i ^ 1 << stride) for i in range(lax.axis_s...]
    pallas_call x0 -> x1, Pallas kernels: none -> 168 us  [body(): pl.pallas_call(kernel, out_shape=jax.ShapeDtypeStruct((SLOTS, TILE, LANES...]
    ppermute x76 -> x0, starting transfers between devices: 156 us -> none  [the longest x70 148 us: from_partner(): lax.ppermute(array, axis, [(i, i ^ 1 << stride) for i in range(lax.axis_s...]
    dot_general x16 -> x0, matrix products: 114 us -> none  [the longest x14 96 us: apply_layer(): summed = jnp.dot(matrix, flat_group, preferred_element_type=jnp.float32)]
    another operation x2 -> x0, local copies, waits for them, and re-layouts: 25.7 us -> none  [permuted_weights(): weights.reshape(blocks, tile_size, fan_count, row_width // fan_count)]
    all_to_all x1 -> x0, blocking collectives: 14.2 us -> none  [body(): lax.all_to_all(results[:, None], 'segment', split_axis=0, concat_axis=1,...]
  transfers between devices with their start and end apart: 76 -> 0, of which waited for: 73 -> 0; matrix products, arithmetic and copies ran while one was open for 7% -> 0% of each run, Pallas kernels for 0% -> 0%
where the time goes in v1:
time: 175 us
  Pallas kernels  168 us (96%)
  local copies, waits for them, and re-layouts  6.03 us (3%)
    pallas_call x1, Pallas kernels, body(): pl.pallas_call(kernel, out_shape=jax.ShapeDtypeStruct((SLOTS, TILE, LANES...  168 us

profile of v1, /device:TPU:26, one launch (start us, length us, event | category | flops | bytes accessed | tf_op | source)
XLA Modules:
  0.0 175.3 jit_solution(3234912289492895781)
XLA Ops:
  0.0 0.8 reshape.12
  0.8 0.3 copy.6
  1.1 1.2 broadcast_in_dim.26
  2.3 1.4 reshape.13.bias
  3.7 0.9 select_reduce_fusion
  4.7 0.7 reshape.11.source
  5.3 168.3 %shard_map.46 = bf16[16,64,128]{2,1,0:T(8,128)(2,1)} custom-call(s32[1024]{0:T(1024)} %reshape.11.source, bf16[2,16,64,2048]{3,2,1,0:T(8,128)(2,1)} %weights.1, f32[2,16,32,128]{3,2,1,0:T(8,128)} %reshape.13.bias, bf16[4,16,64,128]{3,2,1,0:T(8,128)(2,1)} %inputs.1), custom_call_target="tpu_custom_call" | custom-call | tf_op jit(solution)/shard_map/pallas_call | solution.py:365
  173.6 1.7 copy.8

commit v2 on v1

v2 whole, which is shorter than its diff:
```python
import functools

import jax
import jax.numpy as jnp
from jax import lax
from jax.experimental import pallas as pl
from jax.experimental.pallas import tpu as pltpu
from jax.sharding import PartitionSpec as P

MESH = pl.DeviceIdType.MESH
TILE = 64
HALF = 32
FANIN = 32
LANES = 128
SLOTS = 16
ZS = 8
XS = 4
SEGS = 4
MB = 4
CHUNKS = 2 * MB
LAYERS = 2
ORDER = (("enter", 0), ("even", 0), ("spread", 1), ("odd", 2))
COLUMNS = FANIN // 2


def device(segment, x, z, core):
    return {"segment": segment, "blk": (x * ZS + z) * 2 + core}


def low_lanes(shape, width, period):
    lane = lax.broadcasted_iota(jnp.int32, shape, len(shape) - 1)
    return lax.rem(lane, period) < width


def repack(upper, lower):
    low = low_lanes(upper.shape, 64, 128)
    first = jnp.where(low, upper, pltpu.roll(lower, 64, upper.ndim - 1))
    second = jnp.where(low, pltpu.roll(upper, 64, upper.ndim - 1), lower)
    return first, second


def kernel(
    source, weights, bias_rows, inputs, out,
    raw_even, raw_odd, bias, near, far, entering, hidden, landed, odd_in, leaving, final, staged,
    raw_sem, in_sem, entry_recv, entry_send, core_recv, core_send, z_recv, z_send,
    x_recv, x_send, final_recv,
):
    raw = (raw_even, raw_odd)
    segment = lax.axis_index("segment")
    position = lax.axis_index("blk")
    x, z, core = position // (2 * ZS), position // 2 % ZS, position % 2
    upper, inner = x // 2, x % 2
    pair = device(segment, x, z, 1 - core)
    last = segment == SEGS - 1
    first = segment == 0

    def remote(src, dst, send, recv, target):
        return pltpu.make_async_remote_copy(
            src_ref=src, dst_ref=dst, send_sem=send, recv_sem=recv,
            device_id=target, device_id_type=MESH,
        )

    barrier = pltpu.get_barrier_semaphore()

    def greet(target):
        pl.semaphore_signal(barrier, inc=1, device_id=target, device_id_type=MESH)

    greet(pair)
    for step in (2, 1, 3):
        greet(device(segment, (x + step) % XS, z, core))
    for step in (4, 3, 5, 2, 6, 1, 7):
        greet(device(segment, x, (z + step) % ZS, core))

    @pl.when(segment > 0)
    def _():
        for step in (4, 3, 5, 2, 6, 1, 7, 0):
            for other in range(2):
                greet(device(segment - 1, 2 * upper + other, (z + step) % ZS, core))

    def raw_start(layer):
        for column in range(COLUMNS):
            pltpu.make_async_copy(
                weights.at[layer, :, :, pl.ds(column * LANES, LANES)],
                raw[layer].at[:, column], raw_sem.at[layer],
            ).start()

    def raw_copy(layer):
        return pltpu.make_async_copy(
            raw[layer].at[:, pl.ds(COLUMNS, COLUMNS)], raw[layer].at[:, pl.ds(0, COLUMNS)],
            raw_sem.at[layer],
        )

    def in_copy(batch):
        return pltpu.make_async_copy(inputs.at[batch], staged.at[batch], in_sem.at[batch])

    raw_start(0)

    @pl.when(first)
    def _():
        for batch in range(MB):
            in_copy(batch).start()

    raw_start(1)

    def arrange(layer):
        tiles = raw[layer]
        raw_copy(layer).wait()

        def turn(slot, carry):
            for column in range(COLUMNS):
                tiles[slot, COLUMNS + column] = pltpu.roll(tiles[slot, column], 64, 1)
            return carry

        lax.fori_loop(0, SLOTS, turn, 0)

        def one_slot(slot, carry):
            rows = pl.ds(pl.multiple_of(slot * TILE, TILE), TILE)
            low = low_lanes((TILE, LANES), 64, 128)
            quarter = low_lanes((TILE, LANES), 32, 64)
            ours = tiles.at[slot]

            def tile_at(member):
                return ours[source[layer, slot, member]]

            for quad in range(FANIN // 4):
                even = jnp.where(low, tile_at(4 * quad), tile_at(4 * quad + 2))
                odd = jnp.where(low, tile_at(4 * quad + 1), tile_at(4 * quad + 3))
                near[layer, quad, rows] = jnp.where(quarter, even, pltpu.roll(odd, 32, 1))
                far[layer, quad, rows] = jnp.where(quarter, pltpu.roll(even, 96, 1), odd)
            return carry

        lax.fori_loop(0, SLOTS, one_slot, 0)

    low = low_lanes((HALF, LANES), 64, 128)
    for layer in range(LAYERS):
        columns = jnp.transpose(bias_rows[layer], (1, 0))
        for slot in range(SLOTS):
            upper_half = jnp.broadcast_to(columns[:HALF, slot : slot + 1], (HALF, LANES))
            lower_half = jnp.broadcast_to(columns[HALF:, slot : slot + 1], (HALF, LANES))
            bias[layer, slot] = jnp.where(low, upper_half, lower_half)

    arrange(0)

    @pl.when(first)
    def _():
        for batch in range(MB):
            in_copy(batch).wait()

        def pack(step, carry):
            batch, block = step // SLOTS, step % SLOTS
            one, two = repack(
                staged[batch, block, pl.ds(0, HALF), :], staged[batch, block, pl.ds(HALF, HALF), :]
            )
            entering[2 * batch, core, block // ZS, block % ZS] = one
            entering[2 * batch + 1, core, block // ZS, block % ZS] = two
            return carry

        lax.fori_loop(0, MB * SLOTS, pack, 0)

    @pl.when(segment > 0)
    def _():
        arrange(1)

    pl.semaphore_wait(barrier, 11 + jnp.where(last, 0, 16))

    def joined(blocks, layer, rows):
        return jnp.concatenate([blocks[layer, quad, rows] for quad in range(FANIN // 4)], axis=1)

    def multiply(layer, values, block, store):
        rows = pl.ds(pl.multiple_of(block * 4 * TILE, 4 * TILE), 4 * TILE)
        one = jnp.dot(joined(near, layer, rows), values, preferred_element_type=jnp.float32)
        two = jnp.dot(joined(far, layer, rows), values, preferred_element_type=jnp.float32)
        for slot in range(4):
            a, b, c = slot * TILE, slot * TILE + HALF, (slot + 1) * TILE
            kept = jnp.where(low, one[a:b], two[b:c])
            moved = jnp.where(low, one[b:c], two[a:b])
            total = kept + pltpu.roll(moved, 64, 1) + bias[layer, block * 4 + slot]
            store(slot, jnp.maximum(total, 0.0).astype(jnp.bfloat16))

    def quarter_of(group):
        return pl.ds((z // 4 + 1 + group) % 2 * 4, 4)

    def core_copy(chunk, span):
        return remote(
            entering.at[chunk, core, :, span], entering.at[chunk, core, :, span],
            core_send.at[chunk], core_recv.at[chunk], pair,
        )

    def entry_done(chunk, group):
        span = pl.ds(0, 4)
        return remote(
            leaving.at[chunk, :, span], entering.at[chunk, core, :, span],
            entry_send.at[chunk], entry_recv.at[chunk, group], pair,
        )

    def z_done(chunk, group, count):
        span = pl.ds(0, count)
        return remote(
            hidden.at[chunk, :, span], landed.at[chunk, :, span],
            z_send.at[chunk], z_recv.at[chunk, group], pair,
        )

    def x_done(chunk):
        span = pl.ds(0, XS - 1)
        return remote(
            odd_in.at[chunk, span], odd_in.at[chunk, span],
            x_send.at[chunk], x_recv.at[chunk], pair,
        )

    def enter(chunk):
        for group in range(2):
            @pl.when(segment > 0)
            def _():
                entry_done(chunk, group).wait_recv()

            core_copy(chunk, quarter_of(group)).start()

    def even_layer(chunk):
        core_copy(chunk, pl.ds(0, ZS)).wait_recv()
        values = entering[chunk].reshape(FANIN * HALF, LANES)
        for group in range(2):
            part = (z // 4 + 1 + group) % 2
            for other in range(2):
                def store(slot, block):
                    hidden[chunk, other, part * 4 + slot] = block

                multiply(0, values, 2 * other + part, store)
            for step in range(4):
                to = part * 4 + step

                @pl.when(to != z)
                def _():
                    remote(
                        hidden.at[chunk, :, to], landed.at[chunk, :, z],
                        z_send.at[chunk], z_recv.at[chunk, group],
                        device(segment, x, to, core),
                    ).start()

    def spread(chunk):
        for group in range(2):
            z_done(chunk, group, 4 - group).wait_recv()
            if group == 1:
                landed[chunk, :, z] = hidden[chunk, :, z]
            span = quarter_of(group)
            for step in (2, 1, 3):
                to = (x + step) % XS
                remote(
                    landed.at[chunk, to % 2, span], odd_in.at[chunk, x, span],
                    x_send.at[chunk], x_recv.at[chunk], device(segment, to, z, core),
                ).start()
        odd_in[chunk, x] = landed[chunk, inner]

    def odd_layer(chunk):
        x_done(chunk).wait_recv()
        values = odd_in[chunk].reshape(FANIN * HALF, LANES)
        goal = chunk // 2
        for group in range(2):
            part = (z // 4 + 1 + group) % 2
            for other in range(2):
                def store(slot, block):
                    leaving[chunk, other, part * 4 + slot] = block

                multiply(1, values, 2 * other + part, store)
                for step in range(4):
                    to = part * 4 + step
                    block = leaving.at[chunk, other, to]

                    @pl.when(segment < SEGS - 1)
                    def _():
                        remote(
                            block, entering.at[chunk, core, inner, z],
                            entry_send.at[chunk], entry_recv.at[chunk, group],
                            device(segment + 1, 2 * upper + other, to, core),
                        ).start()

                    @pl.when(last)
                    def _():
                        stays = (goal == SEGS - 1) & (to == z) & (other == inner)

                        @pl.when(jnp.logical_not(stays))
                        def _():
                            remote(
                                block, final.at[chunk % 2, inner * ZS + z],
                                entry_send.at[chunk], final_recv.at[chunk % 2],
                                device(goal, 2 * upper + other, to, core),
                            ).start()

        @pl.when(last & (goal == SEGS - 1))
        def _():
            final[chunk % 2, inner * ZS + z] = leaving[chunk, inner, z]

    phases = {"enter": enter, "even": even_layer, "spread": spread, "odd": odd_layer}

    def step(index, carry):
        for name, lag in ORDER:
            chunk = index - lag

            @pl.when((chunk >= 0) & (chunk < CHUNKS))
            def _():
                phases[name](chunk)

            if name == "even":
                @pl.when(first & (chunk == 0))
                def _():
                    arrange(1)

        return carry

    lax.fori_loop(0, CHUNKS + max(lag for _, lag in ORDER), step, 0)

    def final_done(half, count):
        span = pl.ds(0, count)
        return remote(
            final.at[half, span], final.at[half, span],
            entry_send.at[half], final_recv.at[half], pair,
        )

    @pl.when(segment < SEGS - 1)
    def _():
        for half in range(2):
            final_done(half, SLOTS).wait_recv()

    @pl.when(last)
    def _():
        for half in range(2):
            final_done(half, SLOTS - 1).wait_recv()

    def unpack(block, carry):
        one, two = repack(final[0, block], final[1, block])
        out[block, pl.ds(0, HALF), :] = one
        out[block, pl.ds(HALF, HALF), :] = two
        return carry

    lax.fori_loop(0, SLOTS, unpack, 0)

    def drain(chunk, carry):
        core_copy(chunk, pl.ds(0, ZS)).wait_send()
        z_done(chunk, 0, ZS - 1).wait_send()
        x_done(chunk).wait_send()
        whole = jnp.logical_not(last & (chunk // 2 == SEGS - 1))

        @pl.when(whole)
        def _():
            span = pl.ds(0, SLOTS)
            remote(
                final.at[0, span], final.at[0, span],
                entry_send.at[chunk], final_recv.at[0], pair,
            ).wait_send()

        @pl.when(jnp.logical_not(whole))
        def _():
            span = pl.ds(0, SLOTS - 1)
            remote(
                final.at[0, span], final.at[0, span],
                entry_send.at[chunk], final_recv.at[0], pair,
            ).wait_send()

        return carry

    lax.fori_loop(0, CHUNKS, drain, 0)


def body(inputs, weights, biases, tile_index):
    order = jnp.arange(FANIN, dtype=jnp.int32)
    high = (order // 2) % 2
    place = (order[:, None] + high) % 2 * COLUMNS + order[:, None] // 2
    source = jnp.sum(
        jnp.where(tile_index[..., :, None] == order, place, 0), axis=-2, dtype=jnp.int32
    )
    dma = pltpu.SemaphoreType.DMA
    packed = (HALF, LANES)
    vmem = lambda *shape: pltpu.VMEM(shape, jnp.bfloat16)
    result = pl.pallas_call(
        kernel,
        out_shape=jax.ShapeDtypeStruct((SLOTS, TILE, LANES), jnp.bfloat16),
        in_specs=[
            pl.BlockSpec(memory_space=pltpu.SMEM),
            pl.BlockSpec(memory_space=pl.ANY),
            pl.BlockSpec(memory_space=pltpu.VMEM),
            pl.BlockSpec(memory_space=pl.ANY),
        ],
        out_specs=pl.BlockSpec(memory_space=pltpu.VMEM),
        scratch_shapes=[
            vmem(SLOTS, 2 * COLUMNS, TILE, LANES),
            vmem(SLOTS, 2 * COLUMNS, TILE, LANES),
            pltpu.VMEM((LAYERS, SLOTS, HALF, LANES), jnp.float32),
            vmem(LAYERS, FANIN // 4, SLOTS * TILE, LANES),
            vmem(LAYERS, FANIN // 4, SLOTS * TILE, LANES),
            vmem(CHUNKS, 2, 2, ZS, *packed),
            vmem(CHUNKS, 2, ZS, *packed),
            vmem(CHUNKS, 2, ZS, *packed),
            vmem(CHUNKS, XS, ZS, *packed),
            vmem(CHUNKS, 2, ZS, *packed),
            vmem(2, SLOTS, *packed),
            vmem(MB, SLOTS, TILE, LANES),
            dma((LAYERS,)),
            dma((MB,)),
        ]
        + [
            dma((CHUNKS, 2)), dma((CHUNKS,)), dma((CHUNKS,)), dma((CHUNKS,)),
            dma((CHUNKS, 2)), dma((CHUNKS,)), dma((CHUNKS,)), dma((CHUNKS,)), dma((2,)),
        ],
        compiler_params=pltpu.CompilerParams(
            has_side_effects=True, collective_id=0, vmem_limit_bytes=60 * 1024 * 1024
        ),
    )(source, weights, biases, inputs)
    return result[None]


def solution(mesh):
    in_specs = (
        P(None, "blk", None, None),
        P("segment", "blk", None, None),
        P("segment", "blk", None),
        P("segment", "blk", None),
    )
    out_specs = P("segment", "blk", None, None)
    return jax.shard_map(body, mesh=mesh, in_specs=in_specs, out_specs=out_specs, check_vma=False)
```

time: 175 us -> 150 us (0.86)
  Pallas kernels: 168 us -> 146 us
  local copies, waits for them, and re-layouts: 6.03 us -> 1.67 us
    pallas_call x1, Pallas kernels: 168 us -> 146 us  [body(): pl.pallas_call(kernel, out_shape=jax.ShapeDtypeStruct((SLOTS, TILE, LANES...]
    reshape x3 -> x0, local copies, waits for them, and re-layouts: 2.85 us -> none  [the longest x1 1.39 us: body(): bias = bias.reshape(LAYERS, SLOTS, HALF, LANES)]
where the time goes in v2:
time: 150 us
  Pallas kernels  146 us (97%)
  local copies, waits for them, and re-layouts  1.67 us (1%)
  other arithmetic  1.62 us (1%)
    pallas_call x1, Pallas kernels, body(): pl.pallas_call(kernel, out_shape=jax.ShapeDtypeStruct((SLOTS, TILE, LANES...  146 us

profile of v2, /device:TPU:26, one launch (start us, length us, event | category | flops | bytes accessed | tf_op | source)
XLA Modules:
  0.0 149.8 jit_solution(12962111817740824360)
XLA Ops:
  0.0 0.1 fusion.2
  0.1 1.5 %select_reduce_fusion.source = s32[2,16,32]{2,1,0:T(8,128)} fusion(s32[32,32]{1,0:T(8,128)S(1)} %fusion.2, s32[2,16,32]{2,1,0:T(8,128)} %param.7), kind=kLoop, calls=%fused_computation | loop fusion | flops 97280 | bytes 12288 | tf_op jit(solution)/shard_map/reduce_sum | solution.py:367
  1.6 146.5 %shard_map.46 = bf16[16,64,128]{2,1,0:T(8,128)(2,1)} custom-call(s32[2,16,32]{2,1,0:T(8,128)} %select_reduce_fusion.source, bf16[2,16,64,2048]{3,2,1,0:T(8,128)(2,1)} %weights.1, f32[2,16,64]{2,1,0:T(8,128)} %bias_rows.1, bf16[4,16,64,128]{3,2,1,0:T(8,128)(2,1)} %inputs.1), custom_call_target="tpu_custom_call" | custom-call | tf_op jit(solution)/shard_map/pallas_call | solution.py:373
  148.1 1.7 %copy.6 = bf16[1,16,64,128]{3,2,1,0:T(8,128)(2,1)} copy(bf16[1,16,64,128]{3,2,1,0:T(8,128)(2,1)} %bitcast.1) | data formatting | bytes 524288
  (1 shorter events, 0.0 us)

commit v3 on v2

--- a/solution.py
+++ b/solution.py
@@ -93,13 +93,12 @@
     def in_copy(batch):
         return pltpu.make_async_copy(inputs.at[batch], staged.at[batch], in_sem.at[batch])
 
-    raw_start(0)
-
     @pl.when(first)
     def _():
         for batch in range(MB):
             in_copy(batch).start()
 
+    raw_start(0)
     raw_start(1)
 
     def arrange(layer):
@@ -138,8 +137,6 @@
             upper_half = jnp.broadcast_to(columns[:HALF, slot : slot + 1], (HALF, LANES))
             lower_half = jnp.broadcast_to(columns[HALF:, slot : slot + 1], (HALF, LANES))
             bias[layer, slot] = jnp.where(low, upper_half, lower_half)
-
-    arrange(0)
 
     @pl.when(first)
     def _():
@@ -156,6 +153,8 @@
             return carry
 
         lax.fori_loop(0, MB * SLOTS, pack, 0)
+
+    arrange(0)
 
     @pl.when(segment > 0)
     def _():
@@ -207,13 +206,17 @@
             x_send.at[chunk], x_recv.at[chunk], pair,
         )
 
+    @pl.when(first)
+    def _():
+        for chunk in range(CHUNKS):
+            core_copy(chunk, pl.ds(0, ZS)).start()
+
     def enter(chunk):
-        for group in range(2):
-            @pl.when(segment > 0)
-            def _():
+        @pl.when(segment > 0)
+        def _():
+            for group in range(2):
                 entry_done(chunk, group).wait_recv()
-
-            core_copy(chunk, quarter_of(group)).start()
+                core_copy(chunk, quarter_of(group)).start()
 
     def even_layer(chunk):
         core_copy(chunk, pl.ds(0, ZS)).wait_recv()

time: 150 us -> 148 us (0.987)
    pallas_call x1, Pallas kernels: 146 us -> 145 us  [body(): pl.pallas_call(kernel, out_shape=jax.ShapeDtypeStruct((SLOTS, TILE, LANES...]
where the time goes in v3:
time: 148 us
  Pallas kernels  145 us (98%)
  local copies, waits for them, and re-layouts  1.67 us (1%)
  other arithmetic  1.62 us (1%)
    pallas_call x1, Pallas kernels, body(): pl.pallas_call(kernel, out_shape=jax.ShapeDtypeStruct((SLOTS, TILE, LANES...  145 us

profile of v3, /device:TPU:26, one launch (start us, length us, event | category | flops | bytes accessed | tf_op | source)
XLA Modules:
  0.0 148.1 jit_solution(1249489573425995890)
XLA Ops:
  0.0 0.1 fusion.2
  0.1 1.5 %select_reduce_fusion.source = s32[2,16,32]{2,1,0:T(8,128)} fusion(s32[32,32]{1,0:T(8,128)S(1)} %fusion.2, s32[2,16,32]{2,1,0:T(8,128)} %param.7), kind=kLoop, calls=%fused_computation | loop fusion | flops 97280 | bytes 12288 | tf_op jit(solution)/shard_map/reduce_sum | solution.py:370
  1.6 144.8 %shard_map.46 = bf16[16,64,128]{2,1,0:T(8,128)(2,1)} custom-call(s32[2,16,32]{2,1,0:T(8,128)} %select_reduce_fusion.source, bf16[2,16,64,2048]{3,2,1,0:T(8,128)(2,1)} %weights.1, f32[2,16,64]{2,1,0:T(8,128)} %bias_rows.1, bf16[4,16,64,128]{3,2,1,0:T(8,128)(2,1)} %inputs.1), custom_call_target="tpu_custom_call" | custom-call | tf_op jit(solution)/shard_map/pallas_call | solution.py:376
  146.5 1.7 %copy.6 = bf16[1,16,64,128]{3,2,1,0:T(8,128)(2,1)} copy(bf16[1,16,64,128]{3,2,1,0:T(8,128)(2,1)} %bitcast.1) | data formatting | bytes 524288
  (1 shorter events, 0.0 us)
